TPU v7x, 256 devices: a whole 4x4x8 slice. The times are simulated.
256 devices in a mesh: seq: 16 (over y, x), exp: 16 (over z, core), dp: 1.
Axes of the slice: x: 4, y: 4, z: 8, core: 2. Of those that a mesh axis runs over, the one named last changes fastest.
Arguments:
- tokens: bfloat16 [16, 64, 64, 1280], P(('dp', 'exp'), 'seq'), may hold values from -6 to 6
- expert_ids: int32 [16, 64, 64, 1], P(('dp', 'exp'), 'seq'), may hold values from 0 to 31; in each aligned block of 256 rows (0 to 255, 256 to 511, ..., all dimensions but the last counted through in order) at most 10 rows name the same one
- gate_values: float32 [16, 64, 64], P(('dp', 'exp'), 'seq'), may hold values from 0.25 to 1
- mixer_gain: float32 [1280], replicated, may hold values from 0.1 to 1.9
- expert_gain: float32 [1280], replicated, may hold values from 0.1 to 1.9
- conv_weight: float32 [3, 3, 1280], replicated, may hold values from -2 to 2
- conv_bias: float32 [1280], replicated, may hold values from -3 to 3
- w_in: bfloat16 [32, 1280, 5120], P('exp', None, 'seq'), may hold values from -0.15625 to 0.15625
- b_in: float32 [32, 5120], P('exp', 'seq'), may hold values from -3 to 3
- w_out: bfloat16 [32, 5120, 1280], P('exp', 'seq'), may hold values from -0.078125 to 0.078125
- b_out: float32 [32, 1280], P('exp'), may hold values from -3 to 3
Outputs:
- result: bfloat16 [16, 64, 64, 1280], P(('dp', 'exp'), 'seq')
Inputs may be any that keep to these rules, and one draw needn't show every extreme that they name: `expert_ids`: among the 256 patches of one image's block of 4 rows (rows k * 4 to k * 4 + 3), no expert is chosen more than 10 times, and in every draw some expert is chosen exactly 10 times in some block.
All inputs are finite; a program needn't handle non-finite values.
Results may differ from a plain program's by a relative error of at most 0.006.
Values may be sent and summed in bfloat16 or wider, within the bound.
No kernel may reach another device: no remote copies, remote signals or barrier semaphores. Data moves between devices by JAX's collectives and lax.ppermute only.
A program may use at most 128 MiB of HBM per device.

v0:
```python
import jax
import jax.numpy as jnp
from jax import lax
from jax.sharding import PartitionSpec as P


def with_halo(cells, sides, width):
    for axis, dim in sides:
        count = lax.axis_size(axis)
        ends = count - 1
        head = lax.slice_in_dim(cells, 0, width, axis=dim)
        tail = lax.slice_in_dim(cells, cells.shape[dim] - width, cells.shape[dim], axis=dim)
        cells = jnp.concatenate(
            [
                lax.ppermute(tail, axis, [(i, (i + 1) % count) for i in range(ends)]),
                cells,
                lax.ppermute(head, axis, [((i + 1) % count, i) for i in range(ends)]),
            ],
            axis=dim,
        )
    return cells


def normalize(values, scales):
    row_mean = jnp.mean(values, axis=-1, keepdims=True)
    centred = values - row_mean
    row_var = jnp.mean(centred * centred, axis=-1, keepdims=True)
    return centred * lax.rsqrt(row_var + 1e-06) * scales


def depthwise(padded, conv_weight, height, width):
    summed = padded[..., 0:height, 0:width, :] * conv_weight[0, 0]
    for row_off in range(3):
        for col_off in range(3):
            if row_off + col_off > 0:
                summed = (
                    summed
                    + padded[..., row_off : row_off + height, col_off : col_off + width, :]
                    * conv_weight[row_off, col_off]
                )
    return summed


def body(
    tokens,
    expert_ids,
    gate_values,
    mixer_gain,
    expert_gain,
    conv_weight,
    conv_bias,
    w_in,
    b_in,
    w_out,
    b_out,
):
    row_count = tokens.shape[1]
    col_count = tokens.shape[2]
    width_d = tokens.shape[3]
    values = tokens[0].astype(jnp.float32)
    normed = normalize(values, mixer_gain).astype(jnp.bfloat16)
    rim_source = tokens[0]
    extended = with_halo(rim_source, (("seq", 0),), 1)
    rim_rows = jnp.concatenate([extended[0:1], extended[row_count + 1 : row_count + 2]], axis=0)
    rim_rows = normalize(rim_rows.astype(jnp.float32), mixer_gain).astype(jnp.bfloat16)
    extended = jnp.concatenate([rim_rows[0:1], normed, rim_rows[1:2]], axis=0)
    padded = jnp.pad(extended.astype(jnp.float32), ((0, 0), (1, 1), (0, 0)))
    mixed = values + depthwise(padded, conv_weight, row_count, col_count) + conv_bias
    tok_rows = row_count * col_count
    expert_in = normalize(mixed, expert_gain).astype(jnp.bfloat16).reshape(tok_rows, width_d)
    per_device = w_in.shape[0]
    holders = lax.axis_size("exp")
    experts = per_device * holders
    slot_count = 5 * tok_rows // (4 * experts)
    route_ids = expert_ids.reshape(tok_rows)
    one_hot = (route_ids[:, None] == jnp.arange(experts, dtype=jnp.int32)[None, :]).astype(
        jnp.float32
    )
    positions = jnp.arange(tok_rows, dtype=jnp.int32)
    below_mask = (positions[:, None] > positions[None, :]).astype(jnp.float32)
    earlier = jnp.dot(below_mask, one_hot, precision=lax.Precision.HIGHEST)
    slot_rank = jnp.sum(earlier * one_hot, axis=1).astype(jnp.int32)
    column = (
        route_ids // per_device * slot_count + slot_rank
    ) * per_device + route_ids % per_device
    dispatch_mask = (
        column[:, None] == jnp.arange(experts * slot_count, dtype=jnp.int32)[None, :]
    ).astype(jnp.bfloat16)
    dispatched = jnp.einsum(
        "tk,td->kd", dispatch_mask, expert_in, preferred_element_type=jnp.float32
    ).astype(jnp.bfloat16)
    dispatched = dispatched.reshape(holders, slot_count, per_device, width_d)
    received = lax.all_to_all(dispatched, "exp", split_axis=0, concat_axis=0, tiled=True)
    gathered = lax.all_gather(received, "seq", axis=0, tiled=True)
    hidden = (
        jnp.einsum("kcjd,jdf->kcjf", gathered, w_in, preferred_element_type=jnp.float32)
        + b_in[None, None]
    )
    hidden = jax.nn.gelu(hidden, approximate=False).astype(jnp.bfloat16)
    summed = lax.psum_scatter(
        jnp.einsum("kcjf,jfd->kcjd", hidden, w_out, preferred_element_type=jnp.float32).astype(
            jnp.bfloat16
        ),
        "seq",
        scatter_dimension=0,
        tiled=True,
    ).astype(jnp.float32)
    back = (summed + b_out[None, None]).astype(jnp.bfloat16)
    returned = lax.all_to_all(back, "exp", split_axis=0, concat_axis=0, tiled=True).reshape(
        experts * slot_count, width_d
    )
    combined = jnp.dot(dispatch_mask, returned, preferred_element_type=jnp.float32)
    result = mixed.reshape(tok_rows, width_d) + gate_values.reshape(tok_rows)[:, None] * combined
    return result.astype(jnp.bfloat16).reshape(tokens.shape)


def solution(mesh):
    in_specs = (
        P(("dp", "exp"), "seq", None, None),
        P(("dp", "exp"), "seq", None, None),
        P(("dp", "exp"), "seq", None),
        P(),
        P(),
        P(),
        P(),
        P("exp", None, "seq"),
        P("exp", "seq"),
        P("exp", "seq", None),
        P("exp", None),
    )
    out_specs = P(("dp", "exp"), "seq", None, None)
    return jax.shard_map(body, mesh=mesh, in_specs=in_specs, out_specs=out_specs, check_vma=False)
```

profile of v0, /device:TPU:1, one launch (start us, length us, event | category | flops | bytes accessed | tf_op | source)
XLA Modules:
  0.0 334.6 jit_solution(12479019363799753572)
XLA Ops:
  6.5 1.1 slice_bitcast_fusion.1
  7.7 4.0 %collective-permute-start = (bf16[1,64,1280]{2,1,0:T(8,128)(2,1)S(1)}, bf16[1,64,1280]{2,1,0:T(8,128)(2,1)S(1)}, u32[]{:S(2)}, u32[]{:S(2)}) collective-permute-start(bf16[1,64,1280]{2,1,0:T(8,128)(2,1)S(1)} %get-tuple-element.16), channel_id=1, source_target_pairs={{0,16},{16,32},{32,48},{48,64},{64,80},{80,96},{96,112},{112,128},... | collective-permute-start | bytes 491528 | tf_op jit(solution)/shard_map/ppermute | solution.py:15
  11.7 1.3 collective-permute-start.1
  13.0 1.3 convert_reduce_fusion
  14.2 1.4 fusion.61
  15.6 0.5 broadcast.173
  16.2 1.3 reduce.22
  17.8 1.4 fusion.63
  19.2 1.0 slice_reduce_fusion.8
  20.6 0.9 fusion.84
  21.8 1.7 fusion.119
  24.0 1.4 convolution_convert_fusion
  25.4 2.9 reshape.122
  28.3 33.1 %all_to_all.10 = bf16[16,10,2,1280]{3,2,1,0:T(2,128)(2,1)S(1)} all-to-all(bf16[16,10,2,1280]{3,2,1,0:T(2,128)(2,1)} %reshape.122), channel_id=1, replica_groups=mesh['seq'=16,'exp'=16,'dp'=1] {'exp'}, dimensions={0} | all-to-all | bytes 1638400 | tf_op jit(solution)/shard_map/all_to_all | solution.py:93
  61.4 1.0 copy.19
  62.7 95.3 %all-gather.2.cloned.1.call-done = bf16[256,10,2,1280]{3,0,1,2:T(8,128)(2,1)} async-done(((bf16[16,10,2,1280]{3,0,1,2:T(8,128)(2,1)}), bf16[256,10,2,1280]{3,0,1,2:T(8,128)(2,1)}) %all-gather.2.cloned.1.call-update) | async-done | bytes 13107216 | tf_op jit(solution)/shard_map/all_gather | solution.py:94
  158.0 29.0 %convert_bitcast_fusion = bf16[256,10,2,1280]{3,0,1,2:T(8,128)(2,1)} fusion(bf16[256,10,2,1280]{3,0,1,2:T(8,128)(2,1)} %all-gather.2.cloned.1.call-done, f32[2,320]{1,0:T(2,128)S(1)} %copy-done.6, bf16[2,320,1280]{2,1,0:T(8,128)(2,1)S(1)} %copy-done, bf16[2,1280,320]{1,2,0:T(8,128)(2,1)} %param.18), kind=kOutput, calls=%fused_computation | convolution fusion | flops 8503296000 | bytes 29493760 | tf_op jit(solution)/shard_map/kcjf,jfd->kcjd/dot_general | solution.py:101
  187.0 100.8 %reduce-scatter.2.cloned.1.call-done = bf16[16,10,2,1280]{3,0,1,2:T(8,128)(2,1)} async-done(((bf16[256,10,2,1280]{3,0,1,2:T(8,128)(2,1)}), bf16[16,10,2,1280]{3,0,1,2:T(8,128)(2,1)}) %reduce-scatter.2.cloned.1.call-update) | async-done | bytes 819216 | tf_op jit(solution)/shard_map/reduce_scatter | solution.py:100
  287.8 1.3 add_convert_fusion
  289.1 1.7 copy.20
  290.9 7.9 %all-to-all-start.1 = ((bf16[16,10,2,1280]{3,2,1,0:T(2,128)(2,1)}), bf16[16,10,2,1280]{3,2,1,0:T(2,128)(2,1)}, u32[]{:S(2)}, u32[]{:S(2)}) async-start(bf16[16,10,2,1280]{3,2,1,0:T(2,128)(2,1)} %copy.20), calls=%async_computation.2 | async-start | bytes 1638400 | tf_op jit(solution)/shard_map/all_to_all | solution.py:109
  298.9 23.3 %all-to-all-done.1 = bf16[16,10,2,1280]{3,2,1,0:T(2,128)(2,1)} async-done(((bf16[16,10,2,1280]{3,2,1,0:T(2,128)(2,1)}), bf16[16,10,2,1280]{3,2,1,0:T(2,128)(2,1)}, u32[]{:S(2)}, u32[]{:S(2)}) %all-to-all-start.1) | async-done | bytes 819232 | tf_op jit(solution)/shard_map/all_to_all | solution.py:109
  322.2 3.0 reshape.123
  325.2 2.5 fusion.53
  (36 shorter events, 1.8 us)
Async XLA Ops:
  6.5 151.5 %copy-start = (bf16[2,320,1280]{2,1,0:T(8,128)(2,1)S(1)}, bf16[2,320,1280]{2,1,0:T(8,128)(2,1)}, u32[]{:S(2)}) copy-start(bf16[2,320,1280]{2,1,0:T(8,128)(2,1)} %param.20) | copy-start | bytes 4915204
  6.5 15.2 %copy-start.4 = (f32[1280]{0:T(1024)S(1)}, f32[1280]{0:T(1024)}, u32[]{:S(2)}) copy-start(f32[1280]{0:T(1024)} %param.17) | copy-start | bytes 15364
  6.5 151.5 %all-gather.2.cloned.1.call-start = ((), (), s32[]{:S(2)}) async-start(), calls=%async_computation.3 | async-start | bytes 13926400 | tf_op jit(solution)/shard_map/all_gather | solution.py:94
  7.7 12.5 %collective-permute-start = (bf16[1,64,1280]{2,1,0:T(8,128)(2,1)S(1)}, bf16[1,64,1280]{2,1,0:T(8,128)(2,1)S(1)}, u32[]{:S(2)}, u32[]{:S(2)}) collective-permute-start(bf16[1,64,1280]{2,1,0:T(8,128)(2,1)S(1)} %get-tuple-element.16), channel_id=1, source_target_pairs={{0,16},{16,32},{32,48},{48,64},{64,80},{80,96},{96,112},{112,128},... | collective-permute-start | bytes 491528 | tf_op jit(solution)/shard_map/ppermute | solution.py:15
  11.7 8.6 %collective-permute-start.1 = (bf16[1,64,1280]{2,1,0:T(8,128)(2,1)S(1)}, bf16[1,64,1280]{2,1,0:T(8,128)(2,1)S(1)}, u32[]{:S(2)}, u32[]{:S(2)}) collective-permute-start(bf16[1,64,1280]{2,1,0:T(8,128)(2,1)S(1)} %get-tuple-element.17), channel_id=1, source_target_pairs={{16,0},{32,16},{48,32},{64,48},{80,64},{96,80},{112,96},{128,112},... | collective-permute-start | bytes 491528 | tf_op jit(solution)/shard_map/ppermute | solution.py:17
  17.6 4.2 %copy-start.1 = (bf16[1,4,64,1280]{3,2,1,0:T(8,128)(2,1)S(1)}, bf16[1,4,64,1280]{3,2,1,0:T(8,128)(2,1)}, u32[]{:S(2)}) copy-start(bf16[1,4,64,1280]{3,2,1,0:T(8,128)(2,1)} %param.11) | copy-start | bytes 1966084
  21.5 2.2 copy-start.3
  23.4 134.6 %copy-start.6 = (f32[2,320]{1,0:T(2,128)S(1)}, f32[2,320]{1,0:T(2,128)}, u32[]{:S(2)}) copy-start(f32[2,320]{1,0:T(2,128)} %param.19) | copy-start | bytes 7684
  62.5 225.4 %reduce-scatter.2.cloned.1.call-start = ((), (), s32[]{:S(2)}) async-start(), calls=%async_computation.4 | async-start | bytes 13926400 | tf_op jit(solution)/shard_map/reduce_scatter | solution.py:100
  187.0 100.9 %copy-start.2 = (f32[2,1280]{1,0:T(2,128)S(1)}, f32[2,1280]{1,0:T(2,128)}, u32[]{:S(2)}) copy-start(f32[2,1280]{1,0:T(2,128)} %param.21) | copy-start | bytes 30724
  187.0 111.8 %copy-start.5 = (f32[1,4,64]{2,1,0:T(4,128)S(1)}, f32[1,4,64]{2,1,0:T(4,128)}, u32[]{:S(2)}) copy-start(f32[1,4,64]{2,1,0:T(4,128)} %param.13) | copy-start | bytes 3076
  290.9 31.3 %all-to-all-start.1 = ((bf16[16,10,2,1280]{3,2,1,0:T(2,128)(2,1)}), bf16[16,10,2,1280]{3,2,1,0:T(2,128)(2,1)}, u32[]{:S(2)}, u32[]{:S(2)}) async-start(bf16[16,10,2,1280]{3,2,1,0:T(2,128)(2,1)} %copy.20), calls=%async_computation.2 | async-start | bytes 1638400 | tf_op jit(solution)/shard_map/all_to_all | solution.py:109
Sparse Core Ops, SparseCore 0:
  62.6 95.3 all-gather.1
  187.1 100.6 reduce-scatter.1
where the time goes:
time: 335 us
  waiting for transfers between devices  220 us (66%)
  matrix products  33.1 us (10%)
  blocking collectives  33.1 us (10%)
  between operations  13.6 us (4%)
  starting transfers between devices  13.4 us (4%)
  local copies, waits for them, and re-layouts  11.6 us (3%)
  other arithmetic  10.4 us (3%)
    reduce_scatter x1, waiting for transfers between devices, body(): lax.psum_scatter(jnp.einsum('kcjf,jfd->kcjd', hidden, w_out, preferred_el...  101 us
    all_gather x1, waiting for transfers between devices, body(): gathered = lax.all_gather(received, 'seq', axis=0, tiled=True)  95.3 us
    all_to_all x1, blocking collectives, body(): lax.all_to_all(dispatched, 'exp', split_axis=0, concat_axis=0, tiled=True)  33.1 us
    dot_general x1, matrix products, body(): jnp.einsum('kcjf,jfd->kcjd', hidden, w_out, preferred_element_type=jnp.fl...  29 us
    all_to_all x1, waiting for transfers between devices, body(): lax.all_to_all(back, 'exp', split_axis=0, concat_axis=0, tiled=True)  23.3 us
    all_to_all x1, starting transfers between devices, body(): lax.all_to_all(back, 'exp', split_axis=0, concat_axis=0, tiled=True)  7.91 us
  transfers between devices with their start and end apart: 5, of which 3 were waited for; matrix products, arithmetic and copies ran while one was open for 2% of the time, Pallas kernels for 0%

commit v1 on v0

--- a/solution.py
+++ b/solution.py
@@ -91,7 +91,9 @@
     ).astype(jnp.bfloat16)
     dispatched = dispatched.reshape(holders, slot_count, per_device, width_d)
     received = lax.all_to_all(dispatched, "exp", split_axis=0, concat_axis=0, tiled=True)
-    gathered = lax.all_gather(received, "seq", axis=0, tiled=True)
+    gathered = jnp.concatenate(
+        lax.all_to_all(jnp.stack([received] * lax.axis_size("seq")), "seq", 0, 0), axis=0
+    )
     hidden = (
         jnp.einsum("kcjd,jdf->kcjf", gathered, w_in, preferred_element_type=jnp.float32)
         + b_in[None, None]

time: 335 us -> 403 us (1.20)
  blocking collectives: 33.1 us -> 190 us
  waiting for transfers between devices: 220 us -> 118 us
  local copies, waits for them, and re-layouts: 11.6 us -> 24.1 us
    all_to_all x0 -> x1, blocking collectives: none -> 157 us  [body(): lax.all_to_all(jnp.stack([received] * lax.axis_size('seq')), 'seq', 0, 0)]
    all_gather x1 -> x0, waiting for transfers between devices: 95.3 us -> none  [body(): gathered = lax.all_gather(received, 'seq', axis=0, tiled=True)]
    another operation x0 -> x1, local copies, waits for them, and re-layouts: none -> 7.28 us  [body(): jnp.stack([received] * lax.axis_size('seq'))]
    reduce_scatter x1, waiting for transfers between devices: 101 us -> 94.8 us  [body(): lax.psum_scatter(jnp.einsum('kcjf,jfd->kcjd', hidden, w_out, preferred_el...]
    all_to_all x0 -> x1, local copies, waits for them, and re-layouts: none -> 5.23 us  [body(): lax.all_to_all(jnp.stack([received] * lax.axis_size('seq')), 'seq', 0, 0)]
  transfers between devices with their start and end apart: 5 -> 4, of which waited for: 3 -> 2; matrix products, arithmetic and copies ran while one was open for 2% -> 2% of each run, Pallas kernels for 0% -> 0%
where the time goes in v1:
time: 403 us; the launch traced here: 402 us
  blocking collectives  190 us (47%)
  waiting for transfers between devices  118 us (29%)
  matrix products  33.1 us (8%)
  local copies, waits for them, and re-layouts  24.1 us (6%)
  between operations  13.5 us (3%)
  starting transfers between devices  13.1 us (3%)
  other arithmetic  10.4 us (3%)
    all_to_all x1, blocking collectives, body(): lax.all_to_all(jnp.stack([received] * lax.axis_size('seq')), 'seq', 0, 0)  157 us
    reduce_scatter x1, waiting for transfers between devices, body(): lax.psum_scatter(jnp.einsum('kcjf,jfd->kcjd', hidden, w_out, preferred_el...  94.8 us
    all_to_all x1, blocking collectives, body(): lax.all_to_all(dispatched, 'exp', split_axis=0, concat_axis=0, tiled=True)  33.1 us
    dot_general x1, matrix products, body(): jnp.einsum('kcjf,jfd->kcjd', hidden, w_out, preferred_element_type=jnp.fl...  28.9 us
    all_to_all x1, waiting for transfers between devices, body(): lax.all_to_all(back, 'exp', split_axis=0, concat_axis=0, tiled=True)  23.3 us
  transfers between devices with their start and end apart: 4, of which 2 were waited for; matrix products, arithmetic and copies ran while one was open for 2% of the time, Pallas kernels for 0%

profile of v1, /device:TPU:1, one launch (start us, length us, event | category | flops | bytes accessed | tf_op | source)
XLA Modules:
  0.0 402.1 jit_solution(15290407687089227919)
XLA Ops:
  6.5 1.1 slice_bitcast_fusion.1
  7.7 4.0 collective-permute-start
  11.7 1.3 collective-permute-start.1
  13.0 1.3 convert_reduce_fusion
  14.2 1.4 fusion.61
  16.2 1.3 reduce.22
  17.8 1.4 fusion.63
  19.2 1.0 slice_reduce_fusion.8
  21.8 1.7 fusion.119
  24.0 1.4 convolution_convert_fusion
  25.4 2.9 reshape.127
  28.3 33.1 %all_to_all.15 = bf16[16,10,2,1280]{3,2,1,0:T(2,128)(2,1)S(1)} all-to-all(bf16[16,10,2,1280]{3,2,1,0:T(2,128)(2,1)} %reshape.127), channel_id=1, replica_groups=mesh['seq'=16,'exp'=16,'dp'=1] {'exp'}, dimensions={0} | all-to-all | bytes 1638400 | tf_op jit(solution)/shard_map/all_to_all | solution.py:93
  61.4 1.0 copy.19
  62.4 7.3 %stack.2 = bf16[16,16,10,2,1280]{4,1,2,3,0:T(8,128)(2,1)} broadcast(bf16[16,10,2,1280]{3,0,1,2:T(8,128)(2,1)} %copy.19), dimensions={1,2,3,4} | broadcast | bytes 13926400 | tf_op jit(solution)/shard_map/stack | solution.py:95
  69.7 156.6 %all_to_all.16 = bf16[16,16,10,2,1280]{4,1,2,3,0:T(8,128)(2,1)S(1)} all-to-all(bf16[16,16,10,2,1280]{4,1,2,3,0:T(8,128)(2,1)} %stack.2), channel_id=1, replica_groups=mesh['seq'=16,'exp'=16,'dp'=1] {'seq'}, dimensions={0} | all-to-all | bytes 26214400 | tf_op jit(solution)/shard_map/all_to_all | solution.py:95
  226.3 5.2 %copy.20 = bf16[16,16,10,2,1280]{4,1,0,2,3:T(8,128)(2,1)} copy(bf16[16,16,10,2,1280]{4,1,2,3,0:T(8,128)(2,1)S(1)} %all_to_all.16) | data formatting | bytes 26214400 | tf_op jit(solution)/shard_map/all_to_all | solution.py:95
  231.5 28.9 %convert_bitcast_fusion = bf16[256,10,2,1280]{3,0,1,2:T(8,128)(2,1)} fusion(bf16[256,10,2,1280]{3,0,1,2:T(8,128)(2,1)} %bitcast.110, f32[2,320]{1,0:T(2,128)S(1)} %copy-done.7, bf16[2,320,1280]{2,1,0:T(8,128)(2,1)S(1)} %copy-done, bf16[2,1280,320]{1,2,0:T(8,128)(2,1)} %param.18), kind=kOutput, calls=%fused_computation | convolution fusion | flops 8503296000 | bytes 29493760 | tf_op jit(solution)/shard_map/kcjf,jfd->kcjd/dot_general | solution.py:103
  260.5 94.8 %reduce-scatter.2.cloned.1.call-done = bf16[16,10,2,1280]{3,0,1,2:T(8,128)(2,1)} async-done(((bf16[256,10,2,1280]{3,0,1,2:T(8,128)(2,1)}), bf16[16,10,2,1280]{3,0,1,2:T(8,128)(2,1)}) %reduce-scatter.2.cloned.1.call-update) | async-done | bytes 819216 | tf_op jit(solution)/shard_map/reduce_scatter | solution.py:102
  355.3 1.3 add_convert_fusion
  356.6 1.7 copy.21
  358.4 7.9 %all-to-all-start.2 = ((bf16[16,10,2,1280]{3,2,1,0:T(2,128)(2,1)}), bf16[16,10,2,1280]{3,2,1,0:T(2,128)(2,1)}, u32[]{:S(2)}, u32[]{:S(2)}) async-start(bf16[16,10,2,1280]{3,2,1,0:T(2,128)(2,1)} %copy.21), calls=%async_computation.3 | async-start | bytes 1638400 | tf_op jit(solution)/shard_map/all_to_all | solution.py:111
  366.3 23.3 %all-to-all-done.2 = bf16[16,10,2,1280]{3,2,1,0:T(2,128)(2,1)} async-done(((bf16[16,10,2,1280]{3,2,1,0:T(2,128)(2,1)}), bf16[16,10,2,1280]{3,2,1,0:T(2,128)(2,1)}, u32[]{:S(2)}, u32[]{:S(2)}) %all-to-all-start.2) | async-done | bytes 819232 | tf_op jit(solution)/shard_map/all_to_all | solution.py:111
  389.7 3.0 reshape.129
  392.7 2.5 fusion.53
  (38 shorter events, 3.0 us)
Async XLA Ops:
  6.5 225.0 %copy-start = (bf16[2,320,1280]{2,1,0:T(8,128)(2,1)S(1)}, bf16[2,320,1280]{2,1,0:T(8,128)(2,1)}, u32[]{:S(2)}) copy-start(bf16[2,320,1280]{2,1,0:T(8,128)(2,1)} %param.20) | copy-start | bytes 4915204
  6.5 15.2 %copy-start.5 = (f32[1280]{0:T(1024)S(1)}, f32[1280]{0:T(1024)}, u32[]{:S(2)}) copy-start(f32[1280]{0:T(1024)} %param.17) | copy-start | bytes 15364
  6.5 348.8 %reduce-scatter.2.cloned.1.call-start = ((), (), s32[]{:S(2)}) async-start(), calls=%async_computation.4 | async-start | bytes 13926400 | tf_op jit(solution)/shard_map/reduce_scatter | solution.py:102
  7.7 12.5 %collective-permute-start = (bf16[1,64,1280]{2,1,0:T(8,128)(2,1)S(1)}, bf16[1,64,1280]{2,1,0:T(8,128)(2,1)S(1)}, u32[]{:S(2)}, u32[]{:S(2)}) collective-permute-start(bf16[1,64,1280]{2,1,0:T(8,128)(2,1)S(1)} %get-tuple-element.16), channel_id=1, source_target_pairs={{0,16},{16,32},{32,48},{48,64},{64,80},{80,96},{96,112},{112,128},... | collective-permute-start | bytes 491528 | tf_op jit(solution)/shard_map/ppermute | solution.py:15
  11.7 8.6 %collective-permute-start.1 = (bf16[1,64,1280]{2,1,0:T(8,128)(2,1)S(1)}, bf16[1,64,1280]{2,1,0:T(8,128)(2,1)S(1)}, u32[]{:S(2)}, u32[]{:S(2)}) collective-permute-start(bf16[1,64,1280]{2,1,0:T(8,128)(2,1)S(1)} %get-tuple-element.17), channel_id=1, source_target_pairs={{16,0},{32,16},{48,32},{64,48},{80,64},{96,80},{112,96},{128,112},... | collective-permute-start | bytes 491528 | tf_op jit(solution)/shard_map/ppermute | solution.py:17
  17.6 4.2 %copy-start.2 = (bf16[1,4,64,1280]{3,2,1,0:T(8,128)(2,1)S(1)}, bf16[1,4,64,1280]{3,2,1,0:T(8,128)(2,1)}, u32[]{:S(2)}) copy-start(bf16[1,4,64,1280]{3,2,1,0:T(8,128)(2,1)} %param.11) | copy-start | bytes 1966084
  21.5 2.2 copy-start.4
  226.3 5.2 %copy-start.7 = (f32[2,320]{1,0:T(2,128)S(1)}, f32[2,320]{1,0:T(2,128)}, u32[]{:S(2)}) copy-start(f32[2,320]{1,0:T(2,128)} %param.19) | copy-start | bytes 7684
  260.5 94.8 %copy-start.3 = (f32[2,1280]{1,0:T(2,128)S(1)}, f32[2,1280]{1,0:T(2,128)}, u32[]{:S(2)}) copy-start(f32[2,1280]{1,0:T(2,128)} %param.21) | copy-start | bytes 30724
  260.5 105.8 %copy-start.6 = (f32[1,4,64]{2,1,0:T(4,128)S(1)}, f32[1,4,64]{2,1,0:T(4,128)}, u32[]{:S(2)}) copy-start(f32[1,4,64]{2,1,0:T(4,128)} %param.13) | copy-start | bytes 3076
  260.5 134.7 %copy-start.1 = (bf16[2,320,1280]{2,1,0:T(8,128)(2,1)S(1)}, bf16[2,320,1280]{2,1,0:T(8,128)(2,1)}, u32[]{:S(2)}) copy-start(bf16[2,320,1280]{2,1,0:T(8,128)(2,1)} %param.20) | copy-start | bytes 4915204
  358.4 31.3 %all-to-all-start.2 = ((bf16[16,10,2,1280]{3,2,1,0:T(2,128)(2,1)}), bf16[16,10,2,1280]{3,2,1,0:T(2,128)(2,1)}, u32[]{:S(2)}, u32[]{:S(2)}) async-start(bf16[16,10,2,1280]{3,2,1,0:T(2,128)(2,1)} %copy.21), calls=%async_computation.3 | async-start | bytes 1638400 | tf_op jit(solution)/shard_map/all_to_all | solution.py:111
Sparse Core Ops, SparseCore 0:
  260.6 94.6 reduce-scatter.1
